TPU v7x, 128 devices: a whole 4x4x4 slice. The times are simulated.
128 devices in a mesh: facet: 32 (over z, y_hi, x), freq: 4 (over y_lo, core).
Axes of the slice: x: 4, y: 4 (y_hi: 2, y_lo: 2; y = y_hi * 2 + y_lo), z: 4, core: 2. Of those that a mesh axis runs over, the one named last changes fastest.
Arguments:
- visibilities: float32 [32, 10, 2, 128, 128], P('facet', None, None, 'freq'), may hold values from -6 to 6
- coords: float32 [32, 10, 3, 128], P('facet'), may hold values from -1500 to 1500, as said below
- corners: int32 [2, 32, 10], replicated, may hold values from 0 to 480
- owners: int32 [2], replicated, may hold values from 0 to 31, as said below
- assign: int32 [32, 20], P('facet'), may hold values from 0 to 19, as said below
- counts: int32 [32], P('facet'), may hold values from 2 to 20, as said below
Outputs:
- dirty: float32 [32, 512, 512], P('facet', 'freq')
Inputs may be any that keep to these rules, and one draw needn't show every extreme that they name: `owners`: the two sets lie in different slots, one of them in the last slot. `assign`: each facet's row is a permutation of the 20 block numbers; only its first counts entries are gridded. `counts`: some facet grids all 20 blocks. `coords`: at every channel, u and v of each row of a block lie within 12 cells of the centre of that block's subgrid.
All inputs are finite; a program needn't handle non-finite values.
Results may differ from a plain program's by a relative error of at most 0.0037.
Values sent between devices are 32-bit elements; how exact they have to be, the bound alone decides.
A program may use at most 64 MiB of HBM per device.

v0:
```python
import math
import jax
import jax.numpy as jnp
from jax import lax
from jax.sharding import PartitionSpec as P

SUB = 32
G = 512
two_pi = 2.0 * math.pi
field_width = 0.02
band_spread = 0.02
batch_items = 8
highest = lax.Precision.HIGHEST


def spread(value, axis, source):
    kept = jnp.where(lax.axis_index(axis) == source, value, 0).astype(value.dtype)
    return lax.psum(kept, axis)


def facet_center(facet_id, facet_total):
    row_total = facet_total // 8
    column = (facet_id % 8).astype(jnp.float32) - 3.5
    row_pos = (facet_id // 8).astype(jnp.float32) - (row_total - 1) / 2.0
    radius = field_width * field_width * (column * column + row_pos * row_pos)
    w_shift = -radius / (1.0 + jnp.sqrt(1.0 - radius))
    return (column, row_pos, w_shift)


def subgrid_tables():
    offsets = jnp.arange(SUB, dtype=jnp.int32) - SUB // 2
    position = offsets.astype(jnp.float32)
    profile = 1.0 - 0.8 * (position / (SUB / 2.0)) ** 2
    taper_square = profile[:, None] * profile[None, :]
    phase_index = offsets[:, None] * offsets[None, :] % SUB
    phase_angle = -two_pi * phase_index.astype(jnp.float32) / SUB
    return (position, taper_square, jnp.cos(phase_angle), jnp.sin(phase_angle))


def image_tables():
    offsets = jnp.arange(G, dtype=jnp.int32) - G // 2
    phase_index = offsets[:, None] * offsets[None, :] % G
    phase_angle = two_pi * phase_index.astype(jnp.float32) / G
    return (jnp.cos(phase_angle), jnp.sin(phase_angle))


def subgrid_terms(
    vis_blocks, coord_blocks, freq_ratio, corner_u, corner_v, column, row_pos, w_shift, tables
):
    position = tables[0]
    item_total = vis_blocks.shape[0]
    scaled = coord_blocks[:, :, None, :] * freq_ratio[None, None, :, None]
    u_cells = scaled[:, 0]
    v_cells = scaled[:, 1]
    w_waves = scaled[:, 2]
    rotation = two_pi * (
        u_cells * column[:, None, None]
        + v_cells * row_pos[:, None, None]
        + w_waves * w_shift[:, None, None]
    )
    rot_real = jnp.cos(rotation)
    rot_imag = jnp.sin(rotation)
    vis_real = vis_blocks[:, 0] * rot_real - vis_blocks[:, 1] * rot_imag
    vis_imag = vis_blocks[:, 0] * rot_imag + vis_blocks[:, 1] * rot_real
    centre_shift = G // 2 - SUB // 2
    delta_u = (u_cells + (centre_shift - corner_u).astype(jnp.float32)[:, None, None]).reshape(
        item_total, 1, -1
    )
    delta_v = (v_cells + (centre_shift - corner_v).astype(jnp.float32)[:, None, None]).reshape(
        item_total, 1, -1
    )
    angle_u = two_pi / SUB * delta_u * position[None, :, None]
    left_factor = jnp.concatenate([jnp.cos(angle_u), jnp.sin(angle_u)], axis=2).astype(jnp.bfloat16)
    angle_v = two_pi / SUB * delta_v * position[None, :, None]
    wave_real = jnp.cos(angle_v)
    wave_imag = jnp.sin(angle_v)
    flat_real = vis_real.reshape(item_total, 1, -1)
    flat_imag = vis_imag.reshape(item_total, 1, -1)
    right_real = flat_real * wave_real - flat_imag * wave_imag
    right_imag = flat_real * wave_imag + flat_imag * wave_real
    upper_rows = jnp.concatenate([right_real, -right_imag], axis=2)
    lower_rows = jnp.concatenate([right_imag, right_real], axis=2)
    right_factor = jnp.concatenate([upper_rows, lower_rows], axis=1).astype(jnp.bfloat16)
    return (left_factor, right_factor)


def subgrid_finish(product, tables):
    taper_square, dft_real, dft_imag = (tables[1], tables[2], tables[3])
    image_real = product[:, :, :SUB] * taper_square
    image_imag = product[:, :, SUB:] * taper_square
    half_real = jnp.einsum("pl,slm->spm", dft_real, image_real, precision=highest) - jnp.einsum(
        "pl,slm->spm", dft_imag, image_imag, precision=highest
    )
    half_imag = jnp.einsum("pl,slm->spm", dft_real, image_imag, precision=highest) + jnp.einsum(
        "pl,slm->spm", dft_imag, image_real, precision=highest
    )
    uv_real = jnp.einsum("spm,qm->spq", half_real, dft_real, precision=highest) - jnp.einsum(
        "spm,qm->spq", half_imag, dft_imag, precision=highest
    )
    uv_imag = jnp.einsum("spm,qm->spq", half_real, dft_imag, precision=highest) + jnp.einsum(
        "spm,qm->spq", half_imag, dft_real, precision=highest
    )
    return jnp.stack([uv_real, uv_imag], axis=1)


def add_pieces(uv_grid, pieces, corner_u, corner_v, weights):
    zero_index = jnp.zeros((), jnp.int32)
    for item in range(batch_items):
        anchor = (zero_index, corner_u[item], corner_v[item])
        current = lax.dynamic_slice(uv_grid, anchor, (2, SUB, SUB))
        uv_grid = lax.dynamic_update_slice(uv_grid, current + pieces[item] * weights[item], anchor)
    return uv_grid


def broadcast_set(visibilities, coords, set_owner):
    return (spread(visibilities, "facet", set_owner), spread(coords, "facet", set_owner))


def grid_items(block_data, list_pair, end_item, count_first, centre_pair, freq_ratio, tables):
    vis_all, coord_all, corner_all = block_data
    first_list, second_list = list_pair
    first_centre, second_centre = centre_pair
    list_length = first_list.shape[0]

    def grid_step(batch_index, grid_pair):
        item_index = batch_index * batch_items + jnp.arange(batch_items, dtype=jnp.int32)
        is_live = item_index < end_item
        is_later = item_index >= count_first
        slot_index = jnp.clip(
            jnp.where(is_later, item_index - count_first, item_index), 0, list_length - 1
        )
        block_index = jnp.where(
            is_later, jnp.take(second_list, slot_index), jnp.take(first_list, slot_index)
        )
        column = jnp.where(is_later, second_centre[0], first_centre[0])
        row_pos = jnp.where(is_later, second_centre[1], first_centre[1])
        w_shift = jnp.where(is_later, second_centre[2], first_centre[2])
        corner_u = jnp.take(corner_all[0], block_index)
        corner_v = jnp.take(corner_all[1], block_index)
        left_factor, right_factor = subgrid_terms(
            jnp.take(vis_all, block_index, axis=0),
            jnp.take(coord_all, block_index, axis=0),
            freq_ratio,
            corner_u,
            corner_v,
            column,
            row_pos,
            w_shift,
            tables,
        )
        product = jnp.einsum(
            "slk,smk->slm", left_factor, right_factor, preferred_element_type=jnp.float32
        )
        pieces = subgrid_finish(product, tables)
        first_weight = jnp.logical_and(is_live, jnp.logical_not(is_later)).astype(jnp.float32)
        return (add_pieces(grid_pair[0], pieces, corner_u, corner_v, first_weight),)

    empty_grid = jnp.zeros((2, G, G), jnp.float32)
    initial = (empty_grid,)
    batch_total = (end_item + batch_items - 1) // batch_items
    return lax.fori_loop(0, batch_total, grid_step, initial)


def on_device(visibilities, coords, corners, owners, assign, counts):
    facet_total = lax.axis_size("facet")
    band_total = lax.axis_size("freq")
    facet_index = lax.axis_index("facet")
    band_index = lax.axis_index("freq")
    local_channels = visibilities.shape[3]
    block_count = visibilities.shape[1]
    block_rows = visibilities.shape[4]
    channel_total = local_channels * band_total
    channel = band_index * local_channels + jnp.arange(local_channels, dtype=jnp.int32)
    freq_ratio = 1.0 + band_spread * channel.astype(jnp.float32) / channel_total
    first_vis, first_coords = broadcast_set(visibilities, coords, owners[0])
    second_vis, second_coords = broadcast_set(visibilities, coords, owners[1])
    vis_all = jnp.concatenate([first_vis, second_vis], axis=0).reshape(
        2 * block_count, 2, local_channels, block_rows
    )
    coord_all = jnp.concatenate([first_coords, second_coords], axis=0).reshape(
        2 * block_count, 3, block_rows
    )
    corner_all = jnp.take(corners, owners, axis=1).reshape(2, 2 * block_count)
    block_data = (vis_all, coord_all, corner_all)
    tables = subgrid_tables()
    own_list = assign[0]
    own_count = counts[0]
    own_centre = facet_center(facet_index, facet_total)
    (uv_grid,) = grid_items(
        block_data,
        (own_list, own_list),
        own_count,
        own_count,
        (own_centre, own_centre),
        freq_ratio,
        tables,
    )
    cos_table, sin_table = image_tables()
    image_scale = 1.0 / (SUB * SUB * math.sqrt(2 * block_count * block_rows * channel_total))
    right_real = jnp.dot(
        uv_grid[0], cos_table, precision=highest, preferred_element_type=jnp.float32
    ) - jnp.dot(uv_grid[1], sin_table, precision=highest, preferred_element_type=jnp.float32)
    right_imag = jnp.dot(
        uv_grid[0], sin_table, precision=highest, preferred_element_type=jnp.float32
    ) + jnp.dot(uv_grid[1], cos_table, precision=highest, preferred_element_type=jnp.float32)
    image_part = lax.psum_scatter(
        (
            jnp.dot(cos_table, right_real, precision=highest, preferred_element_type=jnp.float32)
            - jnp.dot(sin_table, right_imag, precision=highest, preferred_element_type=jnp.float32)
        )
        * image_scale,
        "freq",
        scatter_dimension=0,
        tiled=True,
    )
    return image_part[None]


def solution(mesh):
    placed = (
        P("facet", None, None, "freq", None),
        P("facet", None, None, None),
        P(),
        P(),
        P("facet", None),
        P("facet"),
    )
    return jax.shard_map(
        on_device, mesh=mesh, in_specs=placed, out_specs=P("facet", "freq", None), check_vma=False
    )
```

profile of v0, /device:TPU:1, one launch (start us, length us, event | category | flops | bytes accessed | tf_op | source)
XLA Modules:
  0.0 707.7 jit_solution(16114662937613344052)
XLA Ops:
  6.5 1.4 fusion.197
  9.3 1.9 broadcast_select_fusion.5
  13.3 0.7 broadcast_select_fusion.7
  14.1 159.7 %all-reduce = (f32[1,10,3,128]{3,0,2,1:T(1,128)S(1)}, f32[1,10,3,128]{3,0,2,1:T(1,128)S(1)}) all-reduce(f32[1,10,3,128]{3,0,2,1:T(1,128)S(1)} %get-tuple-element.335, f32[1,10,3,128]{3,0,2,1:T(1,128)S(1)} %get-tuple-element.334), channel_id=1, replica_groups=mesh['facet'=32,'freq'=4] {'facet'}, use_global_device_ids=true, to_apply=%region_3.4 | all-reduce | flops 7680 | bytes 61440 | tf_op jit(solution)/shard_map/psum | solution.py:18
  174.5 0.8 copy.41
  177.9 161.6 %all-reduce.4.cloned.1.call-done = (f32[1,10,2,32,128]{4,3,2,1,0:T(8,128)}, f32[1,10,2,32,128]{4,3,2,1,0:T(8,128)}) async-done(((f32[1,10,2,32,128]{4,3,2,1,0:T(8,128)}, f32[1,10,2,32,128]{4,3,2,1,0:T(8,128)}), (f32[1,10,2,32,128]{4,3,2,1,0:T(8,128)}, f32[1,10,2,32,128]{4,3,2,1,0:T(8,128)})) %all-reduce.4.cloned.1.call-update) | async-done | bytes 655376 | tf_op jit(solution)/shard_map/psum | solution.py:18
  339.5 1.1 pad_maximum_fusion.1
  340.9 287.0 %while.13 = (s32[]{:T(128)}, f32[2,512,512]{2,1,0:T(8,128)S(1)}, s32[]{:T(128)}, s32[2,20]{1,0:T(2,128)}, s32[]{:T(128)}, /*index=5*/s32[20]{0:T(128)S(1)}, f32[...) while((s32[]{:T(128)}, f32[2,512,512]{2,1,0:T(8,128)S(1)}, ...), condition=%wide.region_5.7_spmd.clone.clone.clone, body=%wide.region_4.6_spmd.clone.clone.clone.sunk | while | flops 351148544 | bytes 27451300 | solution.py:161
  343.0 0.8 slice_bitcast_fusion.8
  345.0 1.4 gather_fusion.1
  347.8 0.8 broadcast_select_fusion.14
  349.1 31.2 %fusion.257 = (bf16[8,32,4096]{2,1,0:T(8,128)(2,1)S(1)}, bf16[8,32,4096]{2,1,0:T(8,128)(2,1)S(1)}, bf16[8,32,4096]{2,1,0:T(8,128)(2,1)S(1)}, bf16[8,32,4096]{2,1,0:T(8,128)(2,1)S(1)}, bf16[8,32,4096]{2,1,0:T(8,128)(2,1)S(1)}) fusion(f32[32]{0:T(128)S(1)} %add_convert_fusion.2, f32[8,4096]{1,0:T(8,128)S(1)} %get-tuple-element.475, ...), kind=kLoop, calls=%fused_computation.33.clone.1 | loop fusion | flops 14680064 | bytes 11010176 | tf_op jit(solution)/shard_map/convert.6
  380.3 3.3 fusion.258
  387.4 0.7 fusion.267
  393.7 1.4 dynamic_update_slice.56
  399.7 1.4 dynamic_update_slice.57
  405.1 0.8 fusion.272
  405.8 1.4 dynamic_update_slice.58
  411.0 0.8 fusion.273
  411.7 1.2 dynamic_update_slice.59
  417.5 1.4 dynamic_update_slice.60
  423.4 1.4 dynamic_update_slice.61
  428.3 0.7 fusion.276
  429.0 1.4 dynamic_update_slice.62
  435.2 1.4 dynamic_update_slice.63
  438.7 0.8 slice_bitcast_fusion.8
  440.7 1.4 gather_fusion.1
  443.5 0.8 broadcast_select_fusion.14
  444.8 31.2 %fusion.257 = (bf16[8,32,4096]{2,1,0:T(8,128)(2,1)S(1)}, bf16[8,32,4096]{2,1,0:T(8,128)(2,1)S(1)}, bf16[8,32,4096]{2,1,0:T(8,128)(2,1)S(1)}, bf16[8,32,4096]{2,1,0:T(8,128)(2,1)S(1)}, bf16[8,32,4096]{2,1,0:T(8,128)(2,1)S(1)}) fusion(f32[32]{0:T(128)S(1)} %add_convert_fusion.2, f32[8,4096]{1,0:T(8,128)S(1)} %get-tuple-element.475, ...), kind=kLoop, calls=%fused_computation.33.clone.1 | loop fusion | flops 14680064 | bytes 11010176 | tf_op jit(solution)/shard_map/convert.6
  476.0 3.3 fusion.258
  489.4 1.4 dynamic_update_slice.56
  495.4 1.4 dynamic_update_slice.57
  500.7 0.8 fusion.272
  501.5 1.4 dynamic_update_slice.58
  506.6 0.8 fusion.273
  507.4 1.4 dynamic_update_slice.59
  513.4 1.4 dynamic_update_slice.60
  519.3 1.4 dynamic_update_slice.61
  524.2 0.7 fusion.276
  524.9 1.4 dynamic_update_slice.62
  531.1 1.2 dynamic_update_slice.63
  534.4 0.8 slice_bitcast_fusion.8
  536.4 1.4 gather_fusion.1
  539.2 0.8 broadcast_select_fusion.14
  540.5 31.2 %fusion.257 = (bf16[8,32,4096]{2,1,0:T(8,128)(2,1)S(1)}, bf16[8,32,4096]{2,1,0:T(8,128)(2,1)S(1)}, bf16[8,32,4096]{2,1,0:T(8,128)(2,1)S(1)}, bf16[8,32,4096]{2,1,0:T(8,128)(2,1)S(1)}, bf16[8,32,4096]{2,1,0:T(8,128)(2,1)S(1)}) fusion(f32[32]{0:T(128)S(1)} %add_convert_fusion.2, f32[8,4096]{1,0:T(8,128)S(1)} %get-tuple-element.475, ...), kind=kLoop, calls=%fused_computation.33.clone.1 | loop fusion | flops 14680064 | bytes 11010176 | tf_op jit(solution)/shard_map/convert.6
  571.7 3.3 fusion.258
  585.1 1.4 dynamic_update_slice.56
  591.1 1.4 dynamic_update_slice.57
  596.4 0.8 fusion.272
  597.2 1.4 dynamic_update_slice.58
  602.3 0.8 fusion.273
  603.1 1.2 dynamic_update_slice.59
  608.9 1.4 dynamic_update_slice.60
  614.7 1.4 dynamic_update_slice.61
  619.7 0.7 fusion.276
  620.4 1.4 dynamic_update_slice.62
  626.6 1.2 dynamic_update_slice.63
  628.0 6.5 fusion.151
  634.5 5.7 fusion.153
  640.3 5.9 convolution_add_fusion.2
  646.2 5.8 convolution_subtract_fusion.3
  652.0 5.9 fusion.162
  657.9 7.0 fusion.145
  664.9 35.5 %reduce-scatter.2.cloned.1.call-done = f32[128,512]{1,0:T(8,128)} async-done(((f32[512,512]{1,0:T(8,128)}), f32[128,512]{1,0:T(8,128)}) %reduce-scatter.2.cloned.1.call-update) | async-done | bytes 262160 | tf_op jit(solution)/shard_map/reduce_scatter | solution.py:206
  (142 shorter events, 47.0 us)
Async XLA Ops:
  6.5 333.0 %all-reduce.4.cloned.1.call-start = ((), (), s32[]{:S(2)}) async-start(), calls=%async_computation.2 | async-start | bytes 1310720 | tf_op jit(solution)/shard_map/psum | solution.py:18
  11.2 329.8 %copy-start = (s32[1,20]{1,0:T(1,128)S(1)}, s32[1,20]{1,0:T(1,128)}, u32[]{:S(2)}) copy-start(s32[1,20]{1,0:T(1,128)} %param.14) | copy-start | bytes 244
  11.2 689.2 %reduce-scatter.2.cloned.1.call-start = ((), (), s32[]{:S(2)}) async-start(), calls=%async_computation.1 | async-start | bytes 1310720 | tf_op jit(solution)/shard_map/reduce_scatter | solution.py:206
  343.0 3.7 copy-start.2
  343.0 3.4 copy-start.1
  380.3 3.3 copy-start.3
  438.6 3.7 copy-start.2
  438.7 3.4 copy-start.1
  476.0 3.3 copy-start.3
  534.3 3.7 copy-start.2
  534.4 3.4 copy-start.1
  571.7 3.3 copy-start.3
  628.0 6.5 copy-start.4
Sparse Core Ops, SparseCore 0:
  11.3 328.1 all-reduce.3
  665.1 35.3 reduce-scatter.1
where the time goes:
time: 720 us; the launch traced here: 708 us
  waiting for transfers between devices  197 us (27%)
  blocking collectives  160 us (22%)
  other arithmetic  129 us (18%)
  loops' own time  92.8 us (13%)
  matrix products  57.5 us (8%)
  local copies, waits for them, and re-layouts  55.2 us (8%)
  between operations  16.1 us (2%)
    psum x1, waiting for transfers between devices, spread(): return lax.psum(kept, axis)  162 us
    psum x1, blocking collectives, spread(): return lax.psum(kept, axis)  160 us
    another operation x3, other arithmetic  93.6 us
    another operation x1, loops' own time, grid_items(): return lax.fori_loop(0, batch_total, grid_step, initial)  92.8 us
    reduce_scatter x1, waiting for transfers between devices, on_device(): lax.psum_scatter((jnp.dot(cos_table, right_real, precision=highest, prefe...  35.5 us
    dynamic_update_slice x24, local copies, waits for them, and re-layouts, add_pieces(): lax.dynamic_update_slice(uv_grid, current + pieces[item] * weights[item],...  32.8 us
    add x24, other arithmetic, add_pieces(): current + pieces[item] * weights[item]  16.8 us
  transfers between devices with their start and end apart: 2, of which 2 were waited for; matrix products, arithmetic and copies ran while one was open for 1% of the time, Pallas kernels for 0%

commit v1 on v0

--- a/solution.py
+++ b/solution.py
@@ -15,7 +15,7 @@
 
 def spread(value, axis, source):
     kept = jnp.where(lax.axis_index(axis) == source, value, 0).astype(value.dtype)
-    return lax.psum(kept, axis)
+    return jnp.sum(lax.all_gather(kept, axis), axis=0)
 
 
 def facet_center(facet_id, facet_total):

time: 720 us -> 608 us (0.84)
  waiting for transfers between devices: 197 us -> 81 us
  blocking collectives: 160 us -> 169 us
  other arithmetic: 129 us -> 137 us
    all_gather x0 -> x2, blocking collectives: none -> 169 us  [spread(): return jnp.sum(lax.all_gather(kept, axis), axis=0)]
    psum x1 -> x0, waiting for transfers between devices: 162 us -> none  [spread(): return lax.psum(kept, axis)]
    psum x1 -> x0, blocking collectives: 160 us -> none  [spread(): return lax.psum(kept, axis)]
    all_gather x0 -> x2, waiting for transfers between devices: none -> 62.3 us  [spread(): return jnp.sum(lax.all_gather(kept, axis), axis=0)]
    reduce_scatter x1, waiting for transfers between devices: 35.5 us -> 18 us  [on_device(): lax.psum_scatter((jnp.dot(cos_table, right_real, precision=highest, prefe...]
    reduce_sum x0 -> x4, other arithmetic: none -> 10.6 us  [spread(): return jnp.sum(lax.all_gather(kept, axis), axis=0)]
  transfers between devices with their start and end apart: 2 -> 3, of which waited for: 2 -> 2; matrix products, arithmetic and copies ran while one was open for 1% -> 1% of each run, Pallas kernels for 0% -> 0%
where the time goes in v1:
time: 608 us; the launch traced here: 603 us
  blocking collectives  169 us (28%)
  other arithmetic  137 us (23%)
  loops' own time  92.7 us (15%)
  waiting for transfers between devices  81 us (13%)
  matrix products  57.4 us (9%)
  local copies, waits for them, and re-layouts  49.6 us (8%)
  between operations  15.7 us (3%)
    all_gather x2, blocking collectives, spread(): return jnp.sum(lax.all_gather(kept, axis), axis=0)  169 us
    another operation x3, other arithmetic  93.6 us
    another operation x1, loops' own time, grid_items(): return lax.fori_loop(0, batch_total, grid_step, initial)  92.7 us
    all_gather x2, waiting for transfers between devices, spread(): return jnp.sum(lax.all_gather(kept, axis), axis=0)  62.3 us
    dynamic_update_slice x24, local copies, waits for them, and re-layouts, add_pieces(): lax.dynamic_update_slice(uv_grid, current + pieces[item] * weights[item],...  32.8 us
    reduce_scatter x1, waiting for transfers between devices, on_device(): lax.psum_scatter((jnp.dot(cos_table, right_real, precision=highest, prefe...  18 us
    add x24, other arithmetic, add_pieces(): current + pieces[item] * weights[item]  17 us
  transfers between devices with their start and end apart: 3, of which 2 were waited for; matrix products, arithmetic and copies ran while one was open for 1% of the time, Pallas kernels for 0%

profile of v1, /device:TPU:1, one launch (start us, length us, event | category | flops | bytes accessed | tf_op | source)
XLA Modules:
  0.0 602.6 jit_solution(12152038727339733812)
XLA Ops:
  6.5 1.4 fusion.197
  9.3 1.9 broadcast_select_fusion.5
  12.8 0.7 copy_select_fusion.1
  13.5 89.7 %all-gather = f32[32,10,3,128]{3,2,1,0:T(4,128)S(1)} all-gather(f32[1,10,3,128]{3,2,1,0:T(4,128)S(1)} %get-tuple-element.330), channel_id=2, replica_groups=mesh['facet'=32,'freq'=4] {'facet'}, dimensions={0}, use_global_device_ids=true | all-gather | bytes 506880 | tf_op jit(solution)/shard_map/all_gather | solution.py:18
  103.3 79.4 %all-gather.1 = f32[32,10,3,128]{3,2,1,0:T(4,128)S(1)} all-gather(f32[1,10,3,128]{3,2,1,0:T(4,128)S(1)} %get-tuple-element.331), channel_id=3, replica_groups=mesh['facet'=32,'freq'=4] {'facet'}, dimensions={0}, use_global_device_ids=true | all-gather | bytes 506880 | tf_op jit(solution)/shard_map/all_gather | solution.py:18
  185.1 5.2 reduce.6
  190.3 62.2 %all-gather.9.cloned.1.call-done = f32[32,10,2,32,128]{4,3,2,1,0:T(8,128)} async-done(((f32[1,10,2,32,128]{4,3,2,1,0:T(8,128)}), f32[32,10,2,32,128]{4,3,2,1,0:T(8,128)}) %all-gather.9.cloned.1.call-update) | async-done | bytes 10485776 | tf_op jit(solution)/shard_map/all_gather | solution.py:18
  252.6 5.2 reduce.7
  258.4 282.4 %while.13 = (s32[]{:T(128)}, f32[2,512,512]{2,1,0:T(8,128)S(1)}, s32[]{:T(128)}, s32[2,20]{1,0:T(2,128)S(1)}, s32[]{:T(128)}, /*index=5*/s32[20]{0:T(128)S(1)}, ...) while((s32[]{:T(128)}, f32[2,512,512]{2,1,0:T(8,128)S(1)}, ...), condition=%wide.region_5.7_spmd.clone.clone.clone, body=%wide.region_4.6_spmd.clone.clone.clone.sunk | while | flops 351148544 | bytes 27698452 | solution.py:161
  265.5 31.2 %fusion.257 = (bf16[8,32,4096]{2,1,0:T(8,128)(2,1)S(1)}, bf16[8,32,4096]{2,1,0:T(8,128)(2,1)S(1)}, bf16[8,32,4096]{2,1,0:T(8,128)(2,1)S(1)}, bf16[8,32,4096]{2,1,0:T(8,128)(2,1)S(1)}, bf16[8,32,4096]{2,1,0:T(8,128)(2,1)S(1)}) fusion(f32[32]{0:T(128)S(1)} %add_convert_fusion.2, f32[8,4096]{1,0:T(8,128)S(1)} %get-tuple-element.471, ...), kind=kLoop, calls=%fused_computation.33.clone.1 | loop fusion | flops 14680064 | bytes 11010176 | tf_op jit(solution)/shard_map/convert.6
  296.7 3.3 fusion.258
  303.7 0.7 fusion.267
  309.5 0.7 fusion.270
  310.2 1.4 dynamic_update_slice.56
  315.4 0.7 fusion.271
  316.1 1.4 dynamic_update_slice.57
  321.9 1.4 dynamic_update_slice.58
  327.4 0.8 fusion.273
  328.2 1.2 dynamic_update_slice.59
  333.1 0.8 fusion.274
  333.9 1.4 dynamic_update_slice.60
  339.7 1.4 dynamic_update_slice.61
  345.6 1.4 dynamic_update_slice.62
  350.7 0.7 fusion.277
  351.4 1.4 dynamic_update_slice.63
  359.5 31.2 %fusion.257 = (bf16[8,32,4096]{2,1,0:T(8,128)(2,1)S(1)}, bf16[8,32,4096]{2,1,0:T(8,128)(2,1)S(1)}, bf16[8,32,4096]{2,1,0:T(8,128)(2,1)S(1)}, bf16[8,32,4096]{2,1,0:T(8,128)(2,1)S(1)}, bf16[8,32,4096]{2,1,0:T(8,128)(2,1)S(1)}) fusion(f32[32]{0:T(128)S(1)} %add_convert_fusion.2, f32[8,4096]{1,0:T(8,128)S(1)} %get-tuple-element.471, ...), kind=kLoop, calls=%fused_computation.33.clone.1 | loop fusion | flops 14680064 | bytes 11010176 | tf_op jit(solution)/shard_map/convert.6
  390.7 3.3 fusion.258
  397.7 0.7 fusion.267
  403.5 0.7 fusion.270
  404.2 1.4 dynamic_update_slice.56
  409.4 0.7 fusion.271
  410.1 1.4 dynamic_update_slice.57
  415.9 1.4 dynamic_update_slice.58
  421.4 0.8 fusion.273
  422.1 1.4 dynamic_update_slice.59
  427.3 0.8 fusion.274
  428.1 1.4 dynamic_update_slice.60
  433.9 1.4 dynamic_update_slice.61
  439.7 1.4 dynamic_update_slice.62
  444.9 0.7 fusion.277
  445.6 1.2 dynamic_update_slice.63
  453.5 31.2 %fusion.257 = (bf16[8,32,4096]{2,1,0:T(8,128)(2,1)S(1)}, bf16[8,32,4096]{2,1,0:T(8,128)(2,1)S(1)}, bf16[8,32,4096]{2,1,0:T(8,128)(2,1)S(1)}, bf16[8,32,4096]{2,1,0:T(8,128)(2,1)S(1)}, bf16[8,32,4096]{2,1,0:T(8,128)(2,1)S(1)}) fusion(f32[32]{0:T(128)S(1)} %add_convert_fusion.2, f32[8,4096]{1,0:T(8,128)S(1)} %get-tuple-element.471, ...), kind=kLoop, calls=%fused_computation.33.clone.1 | loop fusion | flops 14680064 | bytes 11010176 | tf_op jit(solution)/shard_map/convert.6
  484.7 3.3 fusion.258
  491.7 0.7 fusion.267
  497.5 0.7 fusion.270
  498.2 1.4 dynamic_update_slice.56
  503.4 0.7 fusion.271
  504.1 1.4 dynamic_update_slice.57
  509.9 1.4 dynamic_update_slice.58
  515.4 0.8 fusion.273
  516.1 1.2 dynamic_update_slice.59
  521.1 0.8 fusion.274
  521.9 1.4 dynamic_update_slice.60
  527.7 1.4 dynamic_update_slice.61
  533.5 1.4 dynamic_update_slice.62
  538.7 0.7 fusion.277
  539.4 1.2 dynamic_update_slice.63
  540.8 6.5 %fusion.151 = f32[512,512]{1,0:T(8,128)S(1)} fusion(f32[2,512,512]{2,1,0:T(8,128)S(1)} %get-tuple-element.113, s32[512]{0:T(512)} %iota_add_fusion.1), kind=kOutput, calls=%fused_computation.214 | convolution fusion | flops 1614282752 | bytes 2101248 | tf_op jit(solution)/shard_map/dot_general | solution.py:203
  547.3 5.7 fusion.153
  553.1 5.9 convolution_add_fusion.2
  559.0 5.8 convolution_subtract_fusion.3
  564.8 5.9 fusion.162
  570.7 7.0 %fusion.145 = f32[512,512]{1,0:T(8,128)} fusion(f32[512,512]{1,0:T(8,128)S(1)} %fusion.162, f32[512,512]{1,0:T(8,128)S(1)} %convolution_add_fusion.2, s32[512]{0:T(512)S(1)} %copy-done.9), kind=kOutput, calls=%fused_computation.206 | convolution fusion | flops 1614807040 | bytes 3147776 | tf_op jit(solution)/shard_map/dot_general | solution.py:209
  577.7 18.0 %reduce-scatter.2.cloned.1.call-done = f32[128,512]{1,0:T(8,128)} async-done(((f32[512,512]{1,0:T(8,128)}), f32[128,512]{1,0:T(8,128)}) %reduce-scatter.2.cloned.1.call-update) | async-done | bytes 262160 | tf_op jit(solution)/shard_map/reduce_scatter | solution.py:206
  (177 shorter events, 44.3 us)
Async XLA Ops:
  6.5 178.6 %all-gather.7.cloned.1.call-start = ((), (), s32[]{:S(2)}) async-start(), calls=%async_computation.2 | async-start | bytes 10813440 | tf_op jit(solution)/shard_map/all_gather | solution.py:18
  9.3 173.6 %copy-start.8 = (s32[2,32,10]{1,0,2:T(2,128)S(1)}, s32[2,32,10]{1,0,2:T(2,128)}, u32[]{:S(2)}) copy-start(s32[2,32,10]{1,0,2:T(2,128)} %param.12) | copy-start | bytes 7684
  9.3 173.7 %copy-start.10 = (s32[2]{0:T(128)S(1)}, s32[2]{0:T(128)}, u32[]{:S(2)}) copy-start(s32[2]{0:T(128)} %param.13) | copy-start | bytes 28
  11.2 241.3 %all-gather.9.cloned.1.call-start = ((), (), s32[]{:S(2)}) async-start(), calls=%async_computation.3 | async-start | bytes 10813440 | tf_op jit(solution)/shard_map/all_gather | solution.py:18
  12.0 583.8 %reduce-scatter.2.cloned.1.call-start = ((), (), s32[]{:S(2)}) async-start(), calls=%async_computation.1 | async-start | bytes 1310720 | tf_op jit(solution)/shard_map/reduce_scatter | solution.py:206
  257.7 0.7 copy-start
  258.9 2.7 copy-start.6
  258.9 4.6 copy-start.1
  260.9 2.6 copy-start.4
  260.9 2.6 copy-start.3
  296.7 3.3 copy-start.5
  302.8 50.0 %copy-start.2 = (f32[20,3,128]{2,1,0:T(4,128)S(1)}, f32[20,3,128]{2,1,0:T(4,128)}, u32[]{:S(2)}) copy-start(f32[20,3,128]{2,1,0:T(4,128)} %copy-done.1) | copy-start | bytes 92164 | tf_op jit(solution)/shard_map/while
  302.8 50.0 %copy-start.7 = (s32[2,20]{1,0:T(2,128)S(1)}, s32[2,20]{1,0:T(2,128)}, u32[]{:S(2)}) copy-start(s32[2,20]{1,0:T(2,128)} %copy-done.6) | copy-start | bytes 484 | tf_op jit(solution)/shard_map/while
  352.9 2.7 copy-start.6
  352.9 4.6 copy-start.1
  354.9 2.6 copy-start.4
  354.9 2.6 copy-start.3
  390.7 3.3 copy-start.5
  396.8 50.0 %copy-start.2 = (f32[20,3,128]{2,1,0:T(4,128)S(1)}, f32[20,3,128]{2,1,0:T(4,128)}, u32[]{:S(2)}) copy-start(f32[20,3,128]{2,1,0:T(4,128)} %copy-done.1) | copy-start | bytes 92164 | tf_op jit(solution)/shard_map/while
  396.8 50.0 %copy-start.7 = (s32[2,20]{1,0:T(2,128)S(1)}, s32[2,20]{1,0:T(2,128)}, u32[]{:S(2)}) copy-start(s32[2,20]{1,0:T(2,128)} %copy-done.6) | copy-start | bytes 484 | tf_op jit(solution)/shard_map/while
  446.8 2.7 copy-start.6
  446.9 4.6 copy-start.1
  448.9 2.6 copy-start.4
  448.9 2.6 copy-start.3
  484.7 3.3 copy-start.5
  490.8 49.8 %copy-start.2 = (f32[20,3,128]{2,1,0:T(4,128)S(1)}, f32[20,3,128]{2,1,0:T(4,128)}, u32[]{:S(2)}) copy-start(f32[20,3,128]{2,1,0:T(4,128)} %copy-done.1) | copy-start | bytes 92164 | tf_op jit(solution)/shard_map/while
  490.8 49.8 %copy-start.7 = (s32[2,20]{1,0:T(2,128)S(1)}, s32[2,20]{1,0:T(2,128)}, u32[]{:S(2)}) copy-start(s32[2,20]{1,0:T(2,128)} %copy-done.6) | copy-start | bytes 484 | tf_op jit(solution)/shard_map/while
  540.8 6.6 %copy-start.9 = (s32[512]{0:T(512)S(1)}, s32[512]{0:T(512)}, u32[]{:S(2)}) copy-start(s32[512]{0:T(512)} %iota_add_fusion.1) | copy-start | bytes 6148
Sparse Core Ops, SparseCore 0:
  11.3 123.1 all-gather.6
  137.6 114.9 all-gather.8
  577.8 17.8 reduce-scatter.1
